TPU v7x, 32 devices: a whole 2x2x4 slice. The times are simulated.
32 devices in a mesh: gx: 8 (over z, core), gy: 4 (over y, x).
Axes of the slice: x: 2, y: 2, z: 4, core: 2. Of those that a mesh axis runs over, the one named last changes fastest.
Arguments:
- grad_pressure: float32 [64, 128, 1024], P('gx', 'gy'), may hold values from -6 to 6
- beta: float32 [3, 64, 128, 1024], P(None, 'gx', 'gy'), may hold values from 0.25 to 4
- tile_rows: int32 [8192], P(('gx', 'gy')), may hold values from 0 to 2047
- tile_owner: int32 [8192, 1], P(('gx', 'gy')), may hold values from 0 to 31; in each aligned block of 256 rows (0 to 255, 256 to 511, ...) at most 8 rows name the same one
- tile_slot: int32 [8192], P(('gx', 'gy')), may hold values from 0 to 255
- face_mask: int32 [8192, 128], P(('gx', 'gy')), may hold values 0 or 1
- heights: float32 [3, 8192, 128], P(None, ('gx', 'gy')), may hold values from -6 to 6
Outputs:
- grad_rhs: float32 [64, 128, 1024], P('gx', 'gy')
- grad_heights: float32 [3, 8192, 128], P(None, ('gx', 'gy'))
Inputs may be any that keep to these rules, and one draw needn't show every extreme that they name: `tile_rows`: each entry indexes a row of 128 cells inside its own device's block. `tile_owner`: among the 256 tiles of one device no owner is named more than 8 times.
All inputs are finite; a program needn't handle non-finite values. No bound on the sum of `face_mask` on one device may be relied on, other than what follows from the above.
Results may differ from a plain program's by a relative error of at most 0.000025.
Values sent between devices are 32-bit elements; how exact they have to be, the bound alone decides.
A program may use at most 192 MiB of HBM per device.

v0:
```python
import math

import jax
import jax.numpy as jnp
from jax import lax
from jax.sharding import PartitionSpec as P

ITERS = 3
STEPS = 4
CAP = 8


LOW_BOUND = 0.1
HIGH_BOUND = 1.9


def from_behind(array, axis, by):
    size = lax.axis_size(axis)
    pairs = [(i, i + by) for i in range(size) if 0 <= i + by < size]
    return lax.ppermute(array, axis, pairs)


def padded_2(cells, sides, width):
    for axis, dim in sides:
        count = lax.axis_size(axis)
        ends = count - 1
        head = lax.slice_in_dim(cells, 0, width, axis=dim)
        tail = lax.slice_in_dim(cells, cells.shape[dim] - width, cells.shape[dim], axis=dim)
        cells = jnp.concatenate(
            [
                lax.ppermute(tail, axis, [(i, (i + 1) % count) for i in range(ends)]),
                cells,
                lax.ppermute(head, axis, [((i + 1) % count, i) for i in range(ends)]),
            ],
            axis=dim,
        )
    return cells


def omega_of(step_index):
    theta = 0.5 * (HIGH_BOUND + LOW_BOUND) + 0.5 * (HIGH_BOUND - LOW_BOUND) * math.cos(
        math.pi * (2 * step_index + 1) / (2 * STEPS)
    )
    return 1.0 / theta


def z_low(field):
    return jnp.concatenate([jnp.zeros_like(field[:, :, :1]), field[:, :, :-1]], axis=2)


def stencil(scaled, padded, coeffs):
    beta_x, low_x, beta_y, low_y, beta_z, low_z, diagonal = coeffs
    up_z = jnp.concatenate([scaled[:, :, 1:], jnp.zeros_like(scaled[:, :, :1])], axis=2)
    beside = beta_x * padded[2:, 1:-1] + low_x * padded[:-2, 1:-1]
    beside = beside + beta_y * padded[1:-1, 2:] + low_y * padded[1:-1, :-2]
    beside = beside + beta_z * up_z + low_z * z_low(scaled)
    return diagonal * scaled - beside


def near_coeffs(beta):
    beta_x, beta_y, beta_z = (beta[0], beta[1], beta[2])
    rim_x = from_behind(beta_x[-1:], "gx", 1)
    low_x = jnp.concatenate([rim_x, beta_x[:-1]], axis=0)
    rim_y = from_behind(beta_y[:, -1:], "gy", 1)
    low_y = jnp.concatenate([rim_y, beta_y[:, :-1]], axis=1)
    low_z = z_low(beta_z)
    diagonal = beta_x + low_x + beta_y + low_y + beta_z + low_z
    return ((beta_x, low_x, beta_y, low_y, beta_z, low_z, diagonal), 1.0 / diagonal)


def cycle_near(adjoint, coeffs, inv_diag):
    increment = jnp.zeros_like(adjoint)
    for step_index in reversed(range(STEPS)):
        scaled = omega_of(step_index) * inv_diag * adjoint
        increment = increment + scaled
        padded = padded_2(scaled, (("gx", 0), ("gy", 1)), 1)
        adjoint = adjoint - stencil(scaled, padded, coeffs)
    return (adjoint, increment)


def pack_jumps(gradient, tile_rows, owner_ids, tile_slot, face_mask, peers):
    flat_rows = gradient.reshape(-1, 128)
    picked = flat_rows[tile_rows] * face_mask.astype(jnp.float32)
    onehot = (owner_ids[:, None] == jnp.arange(peers, dtype=jnp.int32)[None, :]).astype(jnp.int32)
    position = jnp.sum(jnp.cumsum(onehot, axis=0) * onehot, axis=1) - 1
    target = owner_ids * CAP + position
    send_rows = (
        jnp.zeros((peers * CAP, 128), jnp.float32).at[target].set(picked).reshape(peers, CAP, 128)
    )
    send_slots = (
        jnp.zeros((peers * CAP,), jnp.float32)
        .at[target]
        .set(tile_slot.astype(jnp.float32))
        .reshape(peers, CAP)
    )
    return (send_rows, send_slots)


def add_jumps(slot_table, recv_rows, recv_slots):
    slot_ids = recv_slots.reshape(-1).astype(jnp.int32)
    return slot_table.at[slot_ids].add(recv_rows.reshape(-1, 128))


def curvature_back(slot_table, heights):
    slope = 0.5 * (heights[2] - heights[0])
    bend = heights[2] - 2.0 * heights[1] + heights[0]
    denom = 1.0 + slope * slope
    factor = denom ** (-1.5)
    skew_term = -3.0 * slope * bend * denom ** (-2.5)
    return jnp.stack(
        [
            slot_table * (factor - 0.5 * skew_term),
            -2.0 * slot_table * factor,
            slot_table * (factor + 0.5 * skew_term),
        ]
    )


def shards(grad_pressure, beta, tile_rows, tile_owner, tile_slot, face_mask, heights):
    peers = lax.axis_size("gx") * lax.axis_size("gy")
    owner_ids = tile_owner[:, 0]
    coeffs, inv_diag = near_coeffs(beta)
    adjoint = grad_pressure
    grad_rhs = jnp.zeros_like(grad_pressure)
    slot_table = jnp.zeros((heights.shape[1], 128), jnp.float32)
    for cycle_index in range(ITERS):
        adjoint, increment = cycle_near(adjoint, coeffs, inv_diag)
        grad_rhs = grad_rhs + increment
    send_rows, send_slots = pack_jumps(grad_rhs, tile_rows, owner_ids, tile_slot, face_mask, peers)
    recv_rows, recv_slots = (
        lax.all_to_all(send_rows, ("gx", "gy"), split_axis=0, concat_axis=0, tiled=True),
        lax.all_to_all(send_slots, ("gx", "gy"), split_axis=0, concat_axis=0, tiled=True),
    )
    slot_table = add_jumps(slot_table, recv_rows, recv_slots)
    grad_heights = curvature_back(slot_table, heights)
    return (grad_rhs, grad_heights)


def solution(mesh):
    in_specs = (
        P("gx", "gy", None),
        P(None, "gx", "gy", None),
        P(("gx", "gy")),
        P(("gx", "gy"), None),
        P(("gx", "gy")),
        P(("gx", "gy"), None),
        P(None, ("gx", "gy"), None),
    )
    out_specs = (P("gx", "gy", None), P(None, ("gx", "gy"), None))
    return jax.shard_map(shards, mesh=mesh, in_specs=in_specs, out_specs=out_specs, check_vma=False)
```

profile of v0, /device:TPU:0, one launch (start us, length us, event | category | flops | bytes accessed | tf_op | source)
XLA Modules:
  0.0 295.1 jit_solution(10417572872561733803)
XLA Ops:
  2.5 5.0 %collective-permute-start.1 = (f32[8,1,1024]{2,1,0:T(1,128)S(1)}, f32[8,1,1024]{2,1,0:T(1,128)S(1)}, u32[]{:S(2)}, u32[]{:S(2)}) collective-permute-start(f32[8,1,1024]{2,1,0:T(1,128)S(1)} %slice.550), channel_id=1, source_target_pairs={{0,1},{1,2},{2,3},{4,5},{5,6},{6,7},{8,9},{9,10},{10,11},{12,13},{... | collective-permute-start | bytes 98312 | tf_op jit(solution)/shard_map/ppermute | solution.py:20
  12.2 5.6 %collective-permute-start.3 = (f32[1,32,1024]{2,1,0:T(8,128)S(1)}, f32[1,32,1024]{2,1,0:T(8,128)S(1)}, u32[]{:S(2)}, u32[]{:S(2)}) collective-permute-start(f32[1,32,1024]{2,1,0:T(8,128)S(1)} %get-tuple-element.78), channel_id=1, source_target_pairs={{0,4},{4,8},{8,12},{12,16},{16,20},{20,24},{24,28},{1,5},{5,9},{9,... | collective-permute-start | bytes 393224 | tf_op jit(solution)/shard_map/ppermute | solution.py:31
  46.8 6.2 %collective-permute-start.11 = (f32[1,32,1024]{2,1,0:T(8,128)S(1)}, f32[1,32,1024]{2,1,0:T(8,128)S(1)}, u32[]{:S(2)}, u32[]{:S(2)}) collective-permute-start(f32[1,32,1024]{2,1,0:T(8,128)S(1)} %get-tuple-element.70), channel_id=1, source_target_pairs={{0,4},{4,8},{8,12},{12,16},{16,20},{20,24},{24,28},{1,5},{5,9},{9,... | collective-permute-start | bytes 393224 | tf_op jit(solution)/shard_map/ppermute | solution.py:31
  55.3 5.8 %collective-permute-start.13 = (f32[10,1,1024]{2,1,0:T(1,128)S(1)}, f32[10,1,1024]{2,1,0:T(1,128)S(1)}, u32[]{:S(2)}, u32[]{:S(2)}) collective-permute-start(f32[10,1,1024]{2,1,0:T(1,128)S(1)} %get-tuple-element.33), channel_id=1, source_target_pairs={{0,1},{1,2},{2,3},{4,5},{5,6},{6,7},{8,9},{9,10},{10,11},{12,13},{... | collective-permute-start | bytes 122888 | tf_op jit(solution)/shard_map/ppermute | solution.py:31
  67.6 5.9 %collective-permute-start.15 = (f32[1,32,1024]{2,1,0:T(8,128)S(1)}, f32[1,32,1024]{2,1,0:T(8,128)S(1)}, u32[]{:S(2)}, u32[]{:S(2)}) collective-permute-start(f32[1,32,1024]{2,1,0:T(8,128)S(1)} %get-tuple-element.66), channel_id=1, source_target_pairs={{0,4},{4,8},{8,12},{12,16},{16,20},{20,24},{24,28},{1,5},{5,9},{9,... | collective-permute-start | bytes 393224 | tf_op jit(solution)/shard_map/ppermute | solution.py:31
  75.9 5.8 %collective-permute-start.17 = (f32[10,1,1024]{2,1,0:T(1,128)S(1)}, f32[10,1,1024]{2,1,0:T(1,128)S(1)}, u32[]{:S(2)}, u32[]{:S(2)}) collective-permute-start(f32[10,1,1024]{2,1,0:T(1,128)S(1)} %get-tuple-element.31), channel_id=1, source_target_pairs={{0,1},{1,2},{2,3},{4,5},{5,6},{6,7},{8,9},{9,10},{10,11},{12,13},{... | collective-permute-start | bytes 122888 | tf_op jit(solution)/shard_map/ppermute | solution.py:31
  84.0 6.1 %fusion.149 = (f32[8,32,1024]{2,1,0:T(8,128)S(1)}, f32[8,32,1024]{2,1,0:T(8,128)S(1)}) fusion(f32[8,32,1024]{2,1,0:T(8,128)S(1)} %get-tuple-element.13, f32[8,32,1023]{2,1,0:T(8,128)} %get-tuple-element.69, f32[8,32,1023]{2,1,0:T(8,128)S(1)} %get-tuple-element.68, f32[1,32,1024]{2,1,0:T(8,128)} %copy-done.72, ...), kind=kLoop, calls=%fused_computation.304 | loop fusion | flops 18612224 | bytes 20947968 | tf_op jit(solution)/shard_map/mul | solution.py:74
  91.4 6.2 %collective-permute-start.19 = (f32[1,32,1024]{2,1,0:T(8,128)S(1)}, f32[1,32,1024]{2,1,0:T(8,128)S(1)}, u32[]{:S(2)}, u32[]{:S(2)}) collective-permute-start(f32[1,32,1024]{2,1,0:T(8,128)S(1)} %get-tuple-element.62), channel_id=1, source_target_pairs={{0,4},{4,8},{8,12},{12,16},{16,20},{20,24},{24,28},{1,5},{5,9},{9,... | collective-permute-start | bytes 393224 | tf_op jit(solution)/shard_map/ppermute | solution.py:31
  100.0 5.8 %collective-permute-start.21 = (f32[10,1,1024]{2,1,0:T(1,128)S(1)}, f32[10,1,1024]{2,1,0:T(1,128)S(1)}, u32[]{:S(2)}, u32[]{:S(2)}) collective-permute-start(f32[10,1,1024]{2,1,0:T(1,128)S(1)} %get-tuple-element.29), channel_id=1, source_target_pairs={{0,1},{1,2},{2,3},{4,5},{5,6},{6,7},{8,9},{9,10},{10,11},{12,13},{... | collective-permute-start | bytes 122888 | tf_op jit(solution)/shard_map/ppermute | solution.py:31
  110.7 5.7 %collective-permute-start.23 = (f32[1,32,1024]{2,1,0:T(8,128)S(1)}, f32[1,32,1024]{2,1,0:T(8,128)S(1)}, u32[]{:S(2)}, u32[]{:S(2)}) collective-permute-start(f32[1,32,1024]{2,1,0:T(8,128)S(1)} %get-tuple-element.58), channel_id=1, source_target_pairs={{0,4},{4,8},{8,12},{12,16},{16,20},{20,24},{24,28},{1,5},{5,9},{9,... | collective-permute-start | bytes 393224 | tf_op jit(solution)/shard_map/ppermute | solution.py:31
  118.8 5.9 %collective-permute-start.25 = (f32[10,1,1024]{2,1,0:T(1,128)S(1)}, f32[10,1,1024]{2,1,0:T(1,128)S(1)}, u32[]{:S(2)}, u32[]{:S(2)}) collective-permute-start(f32[10,1,1024]{2,1,0:T(1,128)S(1)} %get-tuple-element.27), channel_id=1, source_target_pairs={{0,1},{1,2},{2,3},{4,5},{5,6},{6,7},{8,9},{9,10},{10,11},{12,13},{... | collective-permute-start | bytes 122888 | tf_op jit(solution)/shard_map/ppermute | solution.py:31
  130.7 6.6 %collective-permute-start.27 = (f32[1,32,1024]{2,1,0:T(8,128)}, f32[1,32,1024]{2,1,0:T(8,128)}, u32[]{:S(2)}, u32[]{:S(2)}) collective-permute-start(f32[1,32,1024]{2,1,0:T(8,128)} %get-tuple-element.54), channel_id=1, source_target_pairs={{0,4},{4,8},{8,12},{12,16},{16,20},{20,24},{24,28},{1,5},{5,9},{9,... | collective-permute-start | bytes 393224 | tf_op jit(solution)/shard_map/ppermute | solution.py:31
  142.0 5.8 %collective-permute-start.29 = (f32[10,1,1024]{2,1,0:T(1,128)S(1)}, f32[10,1,1024]{2,1,0:T(1,128)S(1)}, u32[]{:S(2)}, u32[]{:S(2)}) collective-permute-start(f32[10,1,1024]{2,1,0:T(1,128)S(1)} %get-tuple-element.25), channel_id=1, source_target_pairs={{0,1},{1,2},{2,3},{4,5},{5,6},{6,7},{8,9},{9,10},{10,11},{12,13},{... | collective-permute-start | bytes 122888 | tf_op jit(solution)/shard_map/ppermute | solution.py:31
  149.9 6.3 %multiply_multiply_fusion = f32[8,32,1024]{2,1,0:T(8,128)S(1)} fusion(f32[8,32,1023]{2,1,0:T(8,128)S(1)} %get-tuple-element.57, f32[8,32,1023]{2,1,0:T(8,128)S(1)} %get-tuple-element.56, f32[1,32,1024]{2,1,0:T(8,128)} %collective-permute-done.26, f32[8,32,1024]{2,1,0:T(8,128)} %copy-done.25, f32[1,32,1024]{2,1,0:T(8,128)} %collective-permute-done.27, ...), kind=kLoop, calls=%fused_computation.225 | loop fusion | flops 12845056 | bytes 16411648 | tf_op jit(solution)/shard_map/mul | solution.py:74
  159.2 5.8 %collective-permute-start.31 = (f32[1,32,1024]{2,1,0:T(8,128)}, f32[1,32,1024]{2,1,0:T(8,128)}, u32[]{:S(2)}, u32[]{:S(2)}) collective-permute-start(f32[1,32,1024]{2,1,0:T(8,128)} %get-tuple-element.50), channel_id=1, source_target_pairs={{0,4},{4,8},{8,12},{12,16},{16,20},{20,24},{24,28},{1,5},{5,9},{9,... | collective-permute-start | bytes 393224 | tf_op jit(solution)/shard_map/ppermute | solution.py:31
  172.8 5.8 %collective-permute-start.33 = (f32[10,1,1024]{2,1,0:T(1,128)S(1)}, f32[10,1,1024]{2,1,0:T(1,128)S(1)}, u32[]{:S(2)}, u32[]{:S(2)}) collective-permute-start(f32[10,1,1024]{2,1,0:T(1,128)S(1)} %get-tuple-element.23), channel_id=1, source_target_pairs={{0,1},{1,2},{2,3},{4,5},{5,6},{6,7},{8,9},{9,10},{10,11},{12,13},{... | collective-permute-start | bytes 122888 | tf_op jit(solution)/shard_map/ppermute | solution.py:31
  180.6 8.9 %fusion.148 = (f32[8,32,1024]{2,1,0:T(8,128)S(1)}, f32[8,32,1024]{2,1,0:T(8,128)S(1)}) fusion(f32[8,32,1024]{2,1,0:T(8,128)S(1)} %copy-done.15, f32[8,32,1023]{2,1,0:T(8,128)S(1)} %get-tuple-element.53, f32[8,32,1023]{2,1,0:T(8,128)S(1)} %get-tuple-element.52, f32[1,32,1024]{2,1,0:T(8,128)} %collective-permute-done.30, f32[8,32,1024]{2,1,0:T(8,128)} %copy-done.29, ...), kind=kLoop, calls=%fused_computation.303 | loop fusion | flops 18612224 | bytes 20947968 | tf_op jit(solution)/shard_map/mul | solution.py:74
  197.2 5.2 %collective-permute-start.37 = (f32[10,1,1024]{2,1,0:T(1,128)S(1)}, f32[10,1,1024]{2,1,0:T(1,128)S(1)}, u32[]{:S(2)}, u32[]{:S(2)}) collective-permute-start(f32[10,1,1024]{2,1,0:T(1,128)S(1)} %get-tuple-element.21), channel_id=1, source_target_pairs={{0,1},{1,2},{2,3},{4,5},{5,6},{6,7},{8,9},{9,10},{10,11},{12,13},{... | collective-permute-start | bytes 122888 | tf_op jit(solution)/shard_map/ppermute | solution.py:31
  210.0 5.0 %collective-permute-start.39 = (f32[1,32,1024]{2,1,0:T(8,128)}, f32[1,32,1024]{2,1,0:T(8,128)}, u32[]{:S(2)}, u32[]{:S(2)}) collective-permute-start(f32[1,32,1024]{2,1,0:T(8,128)} %get-tuple-element.42), channel_id=1, source_target_pairs={{0,4},{4,8},{8,12},{12,16},{16,20},{20,24},{24,28},{1,5},{5,9},{9,... | collective-permute-start | bytes 393224 | tf_op jit(solution)/shard_map/ppermute | solution.py:31
  217.3 10.7 %all-to-all-start = ((f32[32,1,8]{2,1,0:T(1,128)}), f32[32,1,8]{2,1,0:T(1,128)S(1)}, u32[]{:S(2)}, u32[]{:S(2)}) async-start(f32[32,1,8]{2,1,0:T(1,128)} %bitcast.10), calls=%async_computation | async-start | bytes 32768 | tf_op jit(solution)/shard_map/all_to_all | solution.py:132
  250.0 5.8 %collective-permute-start.45 = (f32[10,1,1024]{2,1,0:T(1,128)S(1)}, f32[10,1,1024]{2,1,0:T(1,128)}, u32[]{:S(2)}, u32[]{:S(2)}) collective-permute-start(f32[10,1,1024]{2,1,0:T(1,128)S(1)} %get-tuple-element.17), channel_id=1, source_target_pairs={{0,1},{1,2},{2,3},{4,5},{5,6},{6,7},{8,9},{9,10},{10,11},{12,13},{... | collective-permute-start | bytes 122888 | tf_op jit(solution)/shard_map/ppermute | solution.py:31
  257.7 12.1 %fusion.8 = f32[8,32,1024]{2,1,0:T(8,128)} fusion(f32[10,1,1024]{2,1,0:T(1,128)} %collective-permute-done.45, f32[1,32,1024]{2,1,0:T(8,128)} %copy-done.70, f32[8,32,1024]{2,1,0:T(8,128)S(1)} %multiply_multiply_fusion.2, f32[1,32,1024]{2,1,0:T(8,128)} %copy-done.71, f32[10,1,1024]{2,1,0:T(1,128)} %collective-permute-done.44, ...), kind=kLoop, calls=%fused_computation.13 | loop fusion | flops 40370176 | bytes 35605504 | tf_op jit(solution)/shard_map/add | solution.py:128
  274.1 10.1 %all-to-all-start.1 = ((f32[32,8,128]{2,1,0:T(8,128)}), f32[32,8,128]{2,1,0:T(8,128)S(1)}, u32[]{:S(2)}, u32[]{:S(2)}) async-start(f32[32,8,128]{2,1,0:T(8,128)} %bitcast.12), calls=%async_computation.1 | async-start | bytes 262144 | tf_op jit(solution)/shard_map/all_to_all | solution.py:131
  284.4 8.2 %all-to-all-done.1 = f32[32,8,128]{2,1,0:T(8,128)S(1)} async-done(((f32[32,8,128]{2,1,0:T(8,128)}), f32[32,8,128]{2,1,0:T(8,128)S(1)}, u32[]{:S(2)}, u32[]{:S(2)}) %all-to-all-start.1) | async-done | bytes 131104 | tf_op jit(solution)/shard_map/all_to_all | solution.py:131
  (318 shorter events, 132.1 us)
Async XLA Ops:
  45.5 7.5 %collective-permute-start.10 = (f32[1,32,1024]{2,1,0:T(8,128)S(1)}, f32[1,32,1024]{2,1,0:T(8,128)S(1)}, u32[]{:S(2)}, u32[]{:S(2)}) collective-permute-start(f32[1,32,1024]{2,1,0:T(8,128)S(1)} %get-tuple-element.71), channel_id=1, source_target_pairs={{4,0},{8,4},{12,8},{16,12},{20,16},{24,20},{28,24},{5,1},{9,5},{13... | collective-permute-start | bytes 393224 | tf_op jit(solution)/shard_map/ppermute | solution.py:33
  54.0 7.5 %collective-permute-start.12 = (f32[10,1,1024]{2,1,0:T(1,128)S(1)}, f32[10,1,1024]{2,1,0:T(1,128)S(1)}, u32[]{:S(2)}, u32[]{:S(2)}) collective-permute-start(f32[10,1,1024]{2,1,0:T(1,128)S(1)} %get-tuple-element.32), channel_id=1, source_target_pairs={{1,0},{2,1},{3,2},{5,4},{6,5},{7,6},{9,8},{10,9},{11,10},{13,12},{... | collective-permute-start | bytes 122888 | tf_op jit(solution)/shard_map/ppermute | solution.py:33
  55.3 7.4 %collective-permute-start.13 = (f32[10,1,1024]{2,1,0:T(1,128)S(1)}, f32[10,1,1024]{2,1,0:T(1,128)S(1)}, u32[]{:S(2)}, u32[]{:S(2)}) collective-permute-start(f32[10,1,1024]{2,1,0:T(1,128)S(1)} %get-tuple-element.33), channel_id=1, source_target_pairs={{0,1},{1,2},{2,3},{4,5},{5,6},{6,7},{8,9},{9,10},{10,11},{12,13},{... | collective-permute-start | bytes 122888 | tf_op jit(solution)/shard_map/ppermute | solution.py:31
  74.6 8.4 %collective-permute-start.16 = (f32[10,1,1024]{2,1,0:T(1,128)S(1)}, f32[10,1,1024]{2,1,0:T(1,128)S(1)}, u32[]{:S(2)}, u32[]{:S(2)}) collective-permute-start(f32[10,1,1024]{2,1,0:T(1,128)S(1)} %get-tuple-element.30), channel_id=1, source_target_pairs={{1,0},{2,1},{3,2},{5,4},{6,5},{7,6},{9,8},{10,9},{11,10},{13,12},{... | collective-permute-start | bytes 122888 | tf_op jit(solution)/shard_map/ppermute | solution.py:33
  75.9 7.4 %collective-permute-start.17 = (f32[10,1,1024]{2,1,0:T(1,128)S(1)}, f32[10,1,1024]{2,1,0:T(1,128)S(1)}, u32[]{:S(2)}, u32[]{:S(2)}) collective-permute-start(f32[10,1,1024]{2,1,0:T(1,128)S(1)} %get-tuple-element.31), channel_id=1, source_target_pairs={{0,1},{1,2},{2,3},{4,5},{5,6},{6,7},{8,9},{9,10},{10,11},{12,13},{... | collective-permute-start | bytes 122888 | tf_op jit(solution)/shard_map/ppermute | solution.py:31
  90.1 7.5 %collective-permute-start.18 = (f32[1,32,1024]{2,1,0:T(8,128)S(1)}, f32[1,32,1024]{2,1,0:T(8,128)S(1)}, u32[]{:S(2)}, u32[]{:S(2)}) collective-permute-start(f32[1,32,1024]{2,1,0:T(8,128)S(1)} %get-tuple-element.63), channel_id=1, source_target_pairs={{4,0},{8,4},{12,8},{16,12},{20,16},{24,20},{28,24},{5,1},{9,5},{13... | collective-permute-start | bytes 393224 | tf_op jit(solution)/shard_map/ppermute | solution.py:33
  98.7 7.5 %collective-permute-start.20 = (f32[10,1,1024]{2,1,0:T(1,128)S(1)}, f32[10,1,1024]{2,1,0:T(1,128)S(1)}, u32[]{:S(2)}, u32[]{:S(2)}) collective-permute-start(f32[10,1,1024]{2,1,0:T(1,128)S(1)} %get-tuple-element.28), channel_id=1, source_target_pairs={{1,0},{2,1},{3,2},{5,4},{6,5},{7,6},{9,8},{10,9},{11,10},{13,12},{... | collective-permute-start | bytes 122888 | tf_op jit(solution)/shard_map/ppermute | solution.py:33
  100.0 7.4 %collective-permute-start.21 = (f32[10,1,1024]{2,1,0:T(1,128)S(1)}, f32[10,1,1024]{2,1,0:T(1,128)S(1)}, u32[]{:S(2)}, u32[]{:S(2)}) collective-permute-start(f32[10,1,1024]{2,1,0:T(1,128)S(1)} %get-tuple-element.29), channel_id=1, source_target_pairs={{0,1},{1,2},{2,3},{4,5},{5,6},{6,7},{8,9},{9,10},{10,11},{12,13},{... | collective-permute-start | bytes 122888 | tf_op jit(solution)/shard_map/ppermute | solution.py:31
  117.5 7.7 %collective-permute-start.24 = (f32[10,1,1024]{2,1,0:T(1,128)S(1)}, f32[10,1,1024]{2,1,0:T(1,128)S(1)}, u32[]{:S(2)}, u32[]{:S(2)}) collective-permute-start(f32[10,1,1024]{2,1,0:T(1,128)S(1)} %get-tuple-element.26), channel_id=1, source_target_pairs={{1,0},{2,1},{3,2},{5,4},{6,5},{7,6},{9,8},{10,9},{11,10},{13,12},{... | collective-permute-start | bytes 122888 | tf_op jit(solution)/shard_map/ppermute | solution.py:33
  129.4 9.9 %collective-permute-start.26 = (f32[1,32,1024]{2,1,0:T(8,128)}, f32[1,32,1024]{2,1,0:T(8,128)}, u32[]{:S(2)}, u32[]{:S(2)}) collective-permute-start(f32[1,32,1024]{2,1,0:T(8,128)} %get-tuple-element.55), channel_id=1, source_target_pairs={{4,0},{8,4},{12,8},{16,12},{20,16},{24,20},{28,24},{5,1},{9,5},{13... | collective-permute-start | bytes 393224 | tf_op jit(solution)/shard_map/ppermute | solution.py:33
  130.7 8.6 %collective-permute-start.27 = (f32[1,32,1024]{2,1,0:T(8,128)}, f32[1,32,1024]{2,1,0:T(8,128)}, u32[]{:S(2)}, u32[]{:S(2)}) collective-permute-start(f32[1,32,1024]{2,1,0:T(8,128)} %get-tuple-element.54), channel_id=1, source_target_pairs={{0,4},{4,8},{8,12},{12,16},{16,20},{20,24},{24,28},{1,5},{5,9},{9,... | collective-permute-start | bytes 393224 | tf_op jit(solution)/shard_map/ppermute | solution.py:31
  140.6 9.2 %collective-permute-start.28 = (f32[10,1,1024]{2,1,0:T(1,128)S(1)}, f32[10,1,1024]{2,1,0:T(1,128)S(1)}, u32[]{:S(2)}, u32[]{:S(2)}) collective-permute-start(f32[10,1,1024]{2,1,0:T(1,128)S(1)} %get-tuple-element.24), channel_id=1, source_target_pairs={{1,0},{2,1},{3,2},{5,4},{6,5},{7,6},{9,8},{10,9},{11,10},{13,12},{... | collective-permute-start | bytes 122888 | tf_op jit(solution)/shard_map/ppermute | solution.py:33
  142.0 7.8 %collective-permute-start.29 = (f32[10,1,1024]{2,1,0:T(1,128)S(1)}, f32[10,1,1024]{2,1,0:T(1,128)S(1)}, u32[]{:S(2)}, u32[]{:S(2)}) collective-permute-start(f32[10,1,1024]{2,1,0:T(1,128)S(1)} %get-tuple-element.25), channel_id=1, source_target_pairs={{0,1},{1,2},{2,3},{4,5},{5,6},{6,7},{8,9},{9,10},{10,11},{12,13},{... | collective-permute-start | bytes 122888 | tf_op jit(solution)/shard_map/ppermute | solution.py:31
  157.9 12.4 %collective-permute-start.30 = (f32[1,32,1024]{2,1,0:T(8,128)}, f32[1,32,1024]{2,1,0:T(8,128)}, u32[]{:S(2)}, u32[]{:S(2)}) collective-permute-start(f32[1,32,1024]{2,1,0:T(8,128)} %get-tuple-element.51), channel_id=1, source_target_pairs={{4,0},{8,4},{12,8},{16,12},{20,16},{24,20},{28,24},{5,1},{9,5},{13... | collective-permute-start | bytes 393224 | tf_op jit(solution)/shard_map/ppermute | solution.py:33
  159.2 11.1 %collective-permute-start.31 = (f32[1,32,1024]{2,1,0:T(8,128)}, f32[1,32,1024]{2,1,0:T(8,128)}, u32[]{:S(2)}, u32[]{:S(2)}) collective-permute-start(f32[1,32,1024]{2,1,0:T(8,128)} %get-tuple-element.50), channel_id=1, source_target_pairs={{0,4},{4,8},{8,12},{12,16},{16,20},{20,24},{24,28},{1,5},{5,9},{9,... | collective-permute-start | bytes 393224 | tf_op jit(solution)/shard_map/ppermute | solution.py:31
  171.5 9.0 %collective-permute-start.32 = (f32[10,1,1024]{2,1,0:T(1,128)S(1)}, f32[10,1,1024]{2,1,0:T(1,128)S(1)}, u32[]{:S(2)}, u32[]{:S(2)}) collective-permute-start(f32[10,1,1024]{2,1,0:T(1,128)S(1)} %get-tuple-element.22), channel_id=1, source_target_pairs={{1,0},{2,1},{3,2},{5,4},{6,5},{7,6},{9,8},{10,9},{11,10},{13,12},{... | collective-permute-start | bytes 122888 | tf_op jit(solution)/shard_map/ppermute | solution.py:33
  172.8 7.7 %collective-permute-start.33 = (f32[10,1,1024]{2,1,0:T(1,128)S(1)}, f32[10,1,1024]{2,1,0:T(1,128)S(1)}, u32[]{:S(2)}, u32[]{:S(2)}) collective-permute-start(f32[10,1,1024]{2,1,0:T(1,128)S(1)} %get-tuple-element.23), channel_id=1, source_target_pairs={{0,1},{1,2},{2,3},{4,5},{5,6},{6,7},{8,9},{9,10},{10,11},{12,13},{... | collective-permute-start | bytes 122888 | tf_op jit(solution)/shard_map/ppermute | solution.py:31
  208.7 19.3 %collective-permute-start.38 = (f32[1,32,1024]{2,1,0:T(8,128)}, f32[1,32,1024]{2,1,0:T(8,128)}, u32[]{:S(2)}, u32[]{:S(2)}) collective-permute-start(f32[1,32,1024]{2,1,0:T(8,128)} %get-tuple-element.43), channel_id=1, source_target_pairs={{4,0},{8,4},{12,8},{16,12},{20,16},{24,20},{28,24},{5,1},{9,5},{13... | collective-permute-start | bytes 393224 | tf_op jit(solution)/shard_map/ppermute | solution.py:33
  210.0 18.1 %collective-permute-start.39 = (f32[1,32,1024]{2,1,0:T(8,128)}, f32[1,32,1024]{2,1,0:T(8,128)}, u32[]{:S(2)}, u32[]{:S(2)}) collective-permute-start(f32[1,32,1024]{2,1,0:T(8,128)} %get-tuple-element.42), channel_id=1, source_target_pairs={{0,4},{4,8},{8,12},{12,16},{16,20},{20,24},{24,28},{1,5},{5,9},{9,... | collective-permute-start | bytes 393224 | tf_op jit(solution)/shard_map/ppermute | solution.py:31
  217.3 56.9 %all-to-all-start = ((f32[32,1,8]{2,1,0:T(1,128)}), f32[32,1,8]{2,1,0:T(1,128)S(1)}, u32[]{:S(2)}, u32[]{:S(2)}) async-start(f32[32,1,8]{2,1,0:T(1,128)} %bitcast.10), calls=%async_computation | async-start | bytes 32768 | tf_op jit(solution)/shard_map/all_to_all | solution.py:132
  229.3 8.4 %collective-permute-start.40 = (f32[10,1,1024]{2,1,0:T(1,128)S(1)}, f32[10,1,1024]{2,1,0:T(1,128)S(1)}, u32[]{:S(2)}, u32[]{:S(2)}) collective-permute-start(f32[10,1,1024]{2,1,0:T(1,128)S(1)} %get-tuple-element.18), channel_id=1, source_target_pairs={{1,0},{2,1},{3,2},{5,4},{6,5},{7,6},{9,8},{10,9},{11,10},{13,12},{... | collective-permute-start | bytes 122888 | tf_op jit(solution)/shard_map/ppermute | solution.py:33
  248.7 8.8 %collective-permute-start.44 = (f32[10,1,1024]{2,1,0:T(1,128)S(1)}, f32[10,1,1024]{2,1,0:T(1,128)}, u32[]{:S(2)}, u32[]{:S(2)}) collective-permute-start(f32[10,1,1024]{2,1,0:T(1,128)S(1)} %get-tuple-element.16), channel_id=1, source_target_pairs={{1,0},{2,1},{3,2},{5,4},{6,5},{7,6},{9,8},{10,9},{11,10},{13,12},{... | collective-permute-start | bytes 122888 | tf_op jit(solution)/shard_map/ppermute | solution.py:33
  250.0 7.6 %collective-permute-start.45 = (f32[10,1,1024]{2,1,0:T(1,128)S(1)}, f32[10,1,1024]{2,1,0:T(1,128)}, u32[]{:S(2)}, u32[]{:S(2)}) collective-permute-start(f32[10,1,1024]{2,1,0:T(1,128)S(1)} %get-tuple-element.17), channel_id=1, source_target_pairs={{0,1},{1,2},{2,3},{4,5},{5,6},{6,7},{8,9},{9,10},{10,11},{12,13},{... | collective-permute-start | bytes 122888 | tf_op jit(solution)/shard_map/ppermute | solution.py:31
  274.1 18.5 %all-to-all-start.1 = ((f32[32,8,128]{2,1,0:T(8,128)}), f32[32,8,128]{2,1,0:T(8,128)S(1)}, u32[]{:S(2)}, u32[]{:S(2)}) async-start(f32[32,8,128]{2,1,0:T(8,128)} %bitcast.12), calls=%async_computation.1 | async-start | bytes 262144 | tf_op jit(solution)/shard_map/all_to_all | solution.py:131
  (112 other events, 1777.5 us)
where the time goes:
time: 297 us; the launch traced here: 295 us
  starting transfers between devices  175 us (59%)
  other arithmetic  66.8 us (22%)
  local copies, waits for them, and re-layouts  26.2 us (9%)
  waiting for transfers between devices  24.3 us (8%)
    ppermute x22, starting transfers between devices, padded_2(): lax.ppermute(tail, axis, [(i, (i + 1) % count) for i in range(ends)])  119 us
    mul x11, other arithmetic, cycle_near(): scaled = omega_of(step_index) * inv_diag * adjoint  39.5 us
    ppermute x22, starting transfers between devices, padded_2(): lax.ppermute(head, axis, [((i + 1) % count, i) for i in range(ends)])  28.9 us
    ppermute x22, waiting for transfers between devices, padded_2(): lax.ppermute(tail, axis, [(i, (i + 1) % count) for i in range(ends)])  15.1 us
    add x1, other arithmetic, shards(): grad_rhs = grad_rhs + increment  12.1 us
    slice x11, local copies, waits for them, and re-layouts, stencil(): scaled[:, :, 1:]  11.4 us
    all_to_all x1, starting transfers between devices, shards(): lax.all_to_all(send_slots, ('gx', 'gy'), split_axis=0, concat_axis=0, til...  10.7 us
    all_to_all x1, starting transfers between devices, shards(): lax.all_to_all(send_rows, ('gx', 'gy'), split_axis=0, concat_axis=0, tile...  10.1 us
  transfers between devices with their start and end apart: 48, of which 17 were waited for; matrix products, arithmetic and copies ran while one was open for 14% of the time, Pallas kernels for 0%

commit v1 on v0

v1 whole, which is shorter than its diff:
```python
import functools
import math

import jax
import jax.numpy as jnp
from jax import lax
from jax.experimental import pallas as pl
from jax.experimental.pallas import tpu as pltpu
from jax.sharding import PartitionSpec as P

ITERS = 3
STEPS = 4
CAP = 8
LANES = 128
ROWS = 8

LOW_BOUND = 0.1
HIGH_BOUND = 1.9

MESH = pl.DeviceIdType.MESH
EXACT = lax.Precision.HIGHEST


def omega_of(step_index):
    theta = 0.5 * (HIGH_BOUND + LOW_BOUND) + 0.5 * (HIGH_BOUND - LOW_BOUND) * math.cos(
        math.pi * (2 * step_index + 1) / (2 * STEPS)
    )
    return 1.0 / theta


def omega_at(step):
    j = STEPS - 1 - step % STEPS
    value = jnp.float32(omega_of(0))
    for index in range(1, STEPS):
        value = jnp.where(j == index, jnp.float32(omega_of(index)), value)
    return value


def kernel(
    n_x, n_y,
    grad_ref, beta_ref, rows_ref, owner_ref, slot_ref, mask_ref, heights_ref,
    out_ref, back_ref,
    coeff, state, halo_x, halo_y, face_y, rim_x, rim_y, rim_face,
    flat, picked, place, send_rows, recv_rows, send_slots, recv_slots,
    rim_send, rim_recv, x_send, x_recv, y_send, y_recv, row_send, row_recv, slot_send, slot_recv,
):
    X, Y, Z = grad_ref.shape
    groups = Y // ROWS
    blocks = Z // LANES
    tiles = rows_ref.shape[0]
    peers = n_x * n_y
    slots = heights_ref.shape[1]
    ix = lax.axis_index("gx")
    iy = lax.axis_index("gy")
    me = ix * n_y + iy
    has_x = (ix > 0, ix < n_x - 1)
    has_y = (iy > 0, iy < n_y - 1)
    at_x = ((ix - 1, iy), (ix + 1, iy))
    at_y = ((ix, iy - 1), (ix, iy + 1))

    rim_x[...] = jnp.zeros_like(rim_x)
    rim_y[...] = jnp.zeros_like(rim_y)
    halo_x[...] = jnp.zeros_like(halo_x)
    halo_y[...] = jnp.zeros_like(halo_y)

    def peer_at(step):
        peer = (me + step) % peers
        return peer, (peer // n_y, peer % n_y)

    barrier = pltpu.get_barrier_semaphore()

    @pl.loop(1, peers)
    def _(step):
        pl.semaphore_signal(barrier, inc=1, device_id=peer_at(step)[1], device_id_type=MESH)

    for x in range(X):
        rim_face[x : x + 1, :] = beta_ref[1, x, Y - 1 : Y, :]

    owner = owner_ref[...]
    peer_ids = lax.broadcasted_iota(jnp.int32, (tiles, peers), 1)
    named = (owner == peer_ids).astype(jnp.float32)
    before = lax.broadcasted_iota(jnp.int32, (tiles, tiles), 0)
    after = lax.broadcasted_iota(jnp.int32, (tiles, tiles), 1)
    earlier = (after < before).astype(jnp.float32)
    counts = jnp.dot(earlier, named, preferred_element_type=jnp.float32, precision=EXACT)
    position = jnp.sum(counts * named, axis=1, keepdims=True)
    target = owner.astype(jnp.float32) * CAP + position
    columns = lax.broadcasted_iota(jnp.int32, (tiles, peers * CAP), 1).astype(jnp.float32)
    place[...] = (target == columns).astype(jnp.float32)
    slot_row = slot_ref[...].astype(jnp.float32)
    slot_column = jnp.sum(jnp.where(before == after, slot_row, 0.0), axis=1, keepdims=True)
    lanes = lax.broadcasted_iota(jnp.int32, (tiles, LANES), 1).astype(jnp.float32)
    spread = jnp.where(position == lanes, slot_column, 0.0)
    slot_rows = lax.dot_general(
        named, spread, (((0,), (0,)), ((), ())), preferred_element_type=jnp.float32, precision=EXACT
    )
    send_slots[...] = slot_rows.reshape(peers, 1, LANES)

    pl.semaphore_wait(barrier, peers - 1)

    def rim_copies():
        return (
            (has_x, pltpu.make_async_remote_copy(
                beta_ref.at[0, X - 1], rim_x, rim_send.at[0], rim_recv.at[0],
                device_id=at_x[1], device_id_type=MESH)),
            (has_y, pltpu.make_async_remote_copy(
                rim_face, rim_y, rim_send.at[1], rim_recv.at[1],
                device_id=at_y[1], device_id_type=MESH)),
        )

    for has, copy in rim_copies():
        @pl.when(has[1])
        def _():
            copy.start()

    def slot_copy(step):
        peer, place_of = peer_at(step)
        return pltpu.make_async_remote_copy(
            send_slots.at[peer], recv_slots.at[me], slot_send.at[peer], slot_recv.at[me],
            device_id=place_of, device_id_type=MESH)

    def row_copy(step):
        peer, place_of = peer_at(step)
        return pltpu.make_async_remote_copy(
            send_rows.at[peer], recv_rows.at[me], row_send.at[peer], row_recv.at[me],
            device_id=place_of, device_id_type=MESH)

    def rows_of(g):
        return pl.ds(g * ROWS, ROWS)

    def x_copy(par, side, g):
        return pltpu.make_async_remote_copy(
            state.at[par, (X - 1) * side, rows_of(g)], halo_x.at[par, 1 - side, rows_of(g)],
            x_send.at[par, side, g], x_recv.at[par, 1 - side, g],
            device_id=at_x[side], device_id_type=MESH)

    def y_copy(par, side):
        return pltpu.make_async_remote_copy(
            face_y.at[par, side], halo_y.at[par, 1 - side],
            y_send.at[par, side], y_recv.at[par, 1 - side],
            device_id=at_y[side], device_id_type=MESH)

    def x_arrival(par, side, g):
        return pltpu.make_async_remote_copy(
            state.at[par, 0, rows_of(g)], halo_x.at[par, side, rows_of(g)],
            x_send.at[par, side, g], x_recv.at[par, side, g],
            device_id=at_x[side], device_id_type=MESH)

    def y_arrival(par, side):
        return pltpu.make_async_remote_copy(
            face_y.at[par, side], halo_y.at[par, side],
            y_send.at[par, side], y_recv.at[par, side],
            device_id=at_y[side], device_id_type=MESH)

    row_ids = lax.broadcasted_iota(jnp.int32, (ROWS, Z), 0)
    z_ids = lax.broadcasted_iota(jnp.int32, (ROWS, Z), 1)

    def from_below(tile, row):
        return jnp.where(row_ids == 0, row, pltpu.roll(tile, 1, 0))

    def from_above(tile, row):
        return jnp.where(row_ids == ROWS - 1, row, pltpu.roll(tile, ROWS - 1, 0))

    first = omega_at(0)

    def prepare(x, g):
        r = slice(g * ROWS, (g + 1) * ROWS)
        up_x, up_y, up_z = beta_ref[0, x, r, :], beta_ref[1, x, r, :], beta_ref[2, x, r, :]
        low_x = rim_x[r, :] if x == 0 else beta_ref[0, x - 1, r, :]
        row = rim_y[x : x + 1, :] if g == 0 else beta_ref[1, x, g * ROWS - 1 : g * ROWS, :]
        low_y = from_below(up_y, row)
        low_z = jnp.where(z_ids == 0, 0.0, pltpu.roll(up_z, 1, 1))
        inv = 1.0 / (up_x + low_x + up_y + low_y + up_z + low_z)
        up_z = jnp.where(z_ids == Z - 1, 0.0, up_z)
        for index, value in enumerate((up_x, low_x, up_y, low_y, up_z, low_z)):
            coeff[index, x, r, :] = value * inv
        value = inv * grad_ref[x, r, :]
        state[0, x, r, :] = value
        out_ref[x, r, :] = first * value
        if g == 0:
            face_y[0, 0, x : x + 1, :] = value[:1, :]
        if g == groups - 1:
            face_y[0, 1, x : x + 1, :] = value[ROWS - 1 :, :]

    for x in range(1, X):
        for g in range(1, groups):
            prepare(x, g)
    (_, rim_x_copy), (_, rim_y_copy) = rim_copies()

    @pl.when(has_x[0])
    def _():
        rim_x_copy.wait_recv()

    for g in range(1, groups):
        prepare(0, g)
        for side in range(2):
            @pl.when(has_x[side])
            def _():
                x_copy(0, side, g).start()

    @pl.when(has_y[0])
    def _():
        rim_y_copy.wait_recv()

    @pl.when(has_y[1])
    def _():
        y_copy(0, 1).start()

    prepare(0, 0)
    prepare(X - 1, 0)
    for side in range(2):
        @pl.when(has_x[side])
        def _():
            x_copy(0, side, 0).start()
    for x in range(1, X - 1):
        prepare(x, 0)

    @pl.when(has_y[0])
    def _():
        y_copy(0, 0).start()

    for has, copy in rim_copies():
        @pl.when(has[1])
        def _():
            copy.wait_send()

    @pl.loop(1, peers)
    def _(step):
        slot_copy(step).start()

    recv_slots[me] = send_slots[me]

    total = ITERS * STEPS

    def update(par, omega, weight, x, g):
        r = slice(g * ROWS, (g + 1) * ROWS)
        s = state[par, x, r, :]
        above_x = halo_x[par, 1, r, :] if x == X - 1 else state[par, x + 1, r, :]
        below_x = halo_x[par, 0, r, :] if x == 0 else state[par, x - 1, r, :]
        if g == groups - 1:
            above_row = halo_y[par, 1, x : x + 1, :]
        else:
            above_row = state[par, x, (g + 1) * ROWS : (g + 1) * ROWS + 1, :]
        if g == 0:
            below_row = halo_y[par, 0, x : x + 1, :]
        else:
            below_row = state[par, x, g * ROWS - 1 : g * ROWS, :]
        beside = coeff[0, x, r, :] * above_x + coeff[1, x, r, :] * below_x
        beside += coeff[2, x, r, :] * from_above(s, above_row)
        beside += coeff[3, x, r, :] * from_below(s, below_row)
        beside += coeff[4, x, r, :] * pltpu.roll(s, Z - 1, 1)
        beside += coeff[5, x, r, :] * pltpu.roll(s, 1, 1)
        value = s + omega * (beside - s)
        state[1 - par, x, r, :] = value
        out_ref[x, r, :] += weight * value
        if g == 0:
            face_y[1 - par, 0, x : x + 1, :] = value[:1, :]
        if g == groups - 1:
            face_y[1 - par, 1, x : x + 1, :] = value[ROWS - 1 :, :]

    def finish_sends(par, go):
        for side in range(2):
            for g in range(groups):
                @pl.when(jnp.logical_and(has_x[side], go))
                def _():
                    x_copy(par, side, g).wait_send()

            @pl.when(jnp.logical_and(has_y[side], go))
            def _():
                y_copy(par, side).wait_send()

    def step_body(step, carry):
        par = step % 2
        omega, weight = omega_at(step), omega_at(step + 1)
        more = step + 2 < total
        finish_sends(1 - par, step > 0)

        def ends(g):
            for side in range(2):
                @pl.when(has_x[side])
                def _():
                    x_arrival(par, side, g).wait_recv()

                update(par, omega, weight, (X - 1) * side, g)

                @pl.when(jnp.logical_and(has_x[side], more))
                def _():
                    x_copy(1 - par, side, g).start()

        for g in range(1, groups - 1):
            ends(g)
        for side, g in ((0, 0), (1, groups - 1)):
            @pl.when(has_y[side])
            def _():
                y_arrival(par, side).wait_recv()

            ends(g)
            for x in range(1, X - 1):
                update(par, omega, weight, x, g)

            @pl.when(jnp.logical_and(has_y[side], more))
            def _():
                y_copy(1 - par, side).start()

        for x in range(1, X - 1):
            for g in range(1, groups - 1):
                update(par, omega, weight, x, g)
        return carry

    lax.fori_loop(0, total - 1, step_body, 0)
    finish_sends((total - 2) % 2, True)

    for x in range(X):
        for b in range(blocks):
            start = (x * blocks + b) * Y
            flat[start : start + Y, :] = out_ref[x, :, b * LANES : (b + 1) * LANES]

    unroll = 8

    @pl.loop(0, tiles // unroll)
    def _(chunk):
        for lane in range(unroll):
            t = chunk * unroll + lane
            row = rows_ref[t]
            x = row // (Y * blocks)
            y = (row // blocks) % Y
            at = (x * blocks + row % blocks) * Y + y
            picked[pl.ds(t, 1), :] = flat[pl.ds(at, 1), :]

    jumps = picked[...] * mask_ref[...].astype(jnp.float32)
    send_rows[...] = lax.dot_general(
        place[...], jumps, (((0,), (0,)), ((), ())),
        preferred_element_type=jnp.float32, precision=EXACT,
    ).reshape(peers, CAP, LANES)

    @pl.loop(1, peers)
    def _(step):
        row_copy(step).start()

    recv_rows[me] = send_rows[me]

    @pl.loop(1, peers)
    def _(step):
        peer, place_of = peer_at(step)
        pltpu.make_async_remote_copy(
            send_slots.at[peer], recv_slots.at[peer], slot_send.at[peer], slot_recv.at[peer],
            device_id=place_of, device_id_type=MESH).wait()

    own = lax.broadcasted_iota(jnp.int32, (peers, CAP, LANES), 1)
    lane_ids = lax.broadcasted_iota(jnp.int32, (peers, CAP, LANES), 2)
    got = jnp.broadcast_to(recv_slots[...], (peers, CAP, LANES))
    slot_of = jnp.sum(jnp.where(own == lane_ids, got, 0.0), axis=2, keepdims=True)
    slot_of = slot_of.reshape(peers * CAP, 1)
    slot_ids = lax.broadcasted_iota(jnp.int32, (peers * CAP, slots), 1).astype(jnp.float32)
    chosen = (slot_of == slot_ids).astype(jnp.float32)

    slope = 0.5 * (heights_ref[2] - heights_ref[0])
    bend = heights_ref[2] - 2.0 * heights_ref[1] + heights_ref[0]
    denom = 1.0 + slope * slope
    factor = 1.0 / (denom * jnp.sqrt(denom))
    skew = -3.0 * slope * bend * factor / denom

    @pl.loop(1, peers)
    def _(step):
        peer, place_of = peer_at(step)
        pltpu.make_async_remote_copy(
            send_rows.at[peer], recv_rows.at[peer], row_send.at[peer], row_recv.at[peer],
            device_id=place_of, device_id_type=MESH).wait()

    table = lax.dot_general(
        chosen, recv_rows[...].reshape(peers * CAP, LANES), (((0,), (0,)), ((), ())),
        preferred_element_type=jnp.float32, precision=EXACT,
    )
    back_ref[0] = table * (factor - 0.5 * skew)
    back_ref[1] = -2.0 * table * factor
    back_ref[2] = table * (factor + 0.5 * skew)


def shards(grad_pressure, beta, tile_rows, tile_owner, tile_slot, face_mask, heights):
    n_x, n_y = lax.axis_size("gx"), lax.axis_size("gy")
    peers = n_x * n_y
    X, Y, Z = grad_pressure.shape
    groups = Y // ROWS
    tiles = tile_rows.shape[0]
    f32 = jnp.float32
    vmem = pl.BlockSpec(memory_space=pltpu.VMEM)
    smem = pl.BlockSpec(memory_space=pltpu.SMEM)
    dma = pltpu.SemaphoreType.DMA
    return pl.pallas_call(
        functools.partial(kernel, n_x, n_y),
        out_shape=(
            jax.ShapeDtypeStruct((X, Y, Z), f32),
            jax.ShapeDtypeStruct(heights.shape, f32),
        ),
        in_specs=[vmem, vmem, smem, vmem, vmem, vmem, vmem],
        out_specs=(vmem, vmem),
        scratch_shapes=[
            pltpu.VMEM((6, X, Y, Z), f32),
            pltpu.VMEM((2, X, Y, Z), f32),
            pltpu.VMEM((2, 2, Y, Z), f32),
            pltpu.VMEM((2, 2, X, Z), f32),
            pltpu.VMEM((2, 2, X, Z), f32),
            pltpu.VMEM((Y, Z), f32),
            pltpu.VMEM((X, Z), f32),
            pltpu.VMEM((X, Z), f32),
            pltpu.VMEM((X * Y * Z // LANES, LANES), f32),
            pltpu.VMEM((tiles, LANES), f32),
            pltpu.VMEM((tiles, peers * CAP), f32),
            pltpu.VMEM((peers, CAP, LANES), f32),
            pltpu.VMEM((peers, CAP, LANES), f32),
            pltpu.VMEM((peers, 1, LANES), f32),
            pltpu.VMEM((peers, 1, LANES), f32),
            dma((2,)),
            dma((2,)),
            dma((2, 2, groups)),
            dma((2, 2, groups)),
            dma((2, 2)),
            dma((2, 2)),
            dma((peers,)),
            dma((peers,)),
            dma((peers,)),
            dma((peers,)),
        ],
        compiler_params=pltpu.CompilerParams(
            collective_id=0, has_side_effects=True, vmem_limit_bytes=56 * 1024 * 1024
        ),
    )(grad_pressure, beta, tile_rows, tile_owner, tile_slot.reshape(1, -1), face_mask, heights)


def solution(mesh):
    in_specs = (
        P("gx", "gy", None),
        P(None, "gx", "gy", None),
        P(("gx", "gy")),
        P(("gx", "gy"), None),
        P(("gx", "gy")),
        P(("gx", "gy"), None),
        P(None, ("gx", "gy"), None),
    )
    out_specs = (P("gx", "gy", None), P(None, ("gx", "gy"), None))
    return jax.shard_map(shards, mesh=mesh, in_specs=in_specs, out_specs=out_specs, check_vma=False)
```

time: 297 us -> 73.7 us (0.25)
  starting transfers between devices: 175 us -> 0 us
  Pallas kernels: 0 us -> 67.3 us
  other arithmetic: 66.8 us -> 0 us
  waiting for transfers between devices: 24.3 us -> 0 us
  local copies, waits for them, and re-layouts: 26.2 us -> 5.55 us
    ppermute x46 -> x0, starting transfers between devices: 154 us -> none  [the longest x22 119 us: padded_2(): lax.ppermute(tail, axis, [(i, (i + 1) % count) for i in range(ends)])]
    pallas_call x0 -> x1, Pallas kernels: none -> 67.3 us  [shards(): pl.pallas_call(functools.partial(kernel, n_x, n_y), out_shape=(jax.ShapeD...]
    mul x11 -> x0, other arithmetic: 39.5 us -> none  [cycle_near(): scaled = omega_of(step_index) * inv_diag * adjoint]
    all_to_all x2 -> x0, starting transfers between devices: 20.8 us -> none  [the longest x1 10.7 us: shards(): lax.all_to_all(send_slots, ('gx', 'gy'), split_axis=0, concat_axis=0, til...]
    ppermute x46 -> x0, waiting for transfers between devices: 16.1 us -> none  [the longest x22 15.1 us: padded_2(): lax.ppermute(tail, axis, [(i, (i + 1) % count) for i in range(ends)])]
    slice x26 -> x0, local copies, waits for them, and re-layouts: 14.6 us -> none  [the longest x11 11.4 us: stencil(): scaled[:, :, 1:]]
    add x1 -> x0, other arithmetic: 12.1 us -> none  [shards(): grad_rhs = grad_rhs + increment]
    all_to_all x2 -> x0, waiting for transfers between devices: 8.22 us -> none  [the longest x1 8.22 us: shards(): lax.all_to_all(send_rows, ('gx', 'gy'), split_axis=0, concat_axis=0, tile...]
  transfers between devices with their start and end apart: 48 -> 0, of which waited for: 17 -> 0; matrix products, arithmetic and copies ran while one was open for 14% -> 0% of each run, Pallas kernels for 0% -> 0%
where the time goes in v1:
time: 73.7 us; the launch traced here: 73.5 us
  Pallas kernels  67.3 us (91%)
  local copies, waits for them, and re-layouts  5.55 us (8%)
    pallas_call x1, Pallas kernels, shards(): pl.pallas_call(functools.partial(kernel, n_x, n_y), out_shape=(jax.ShapeD...  67.3 us
    unnamed x3, local copies, waits for them, and re-layouts  5.55 us

profile of v1, /device:TPU:0, one launch (start us, length us, event | category | flops | bytes accessed | tf_op | source)
XLA Modules:
  0.0 73.5 jit_solution(17395509334036038328)
XLA Ops:
  0.6 1.5 %copy.9.owner_ref = s32[256,1]{1,0:T(8,128)} copy(s32[256,1]{0,1:T(1,128)} %param.10) | data formatting | bytes 2048 | tf_op args[3]
  2.1 67.3 %shard_map.86 = (f32[8,32,1024]{2,1,0:T(8,128)}, f32[3,256,128]{2,1,0:T(8,128)}) custom-call(f32[8,32,1024]{2,1,0:T(8,128)} %grad_ref.1, f32[3,8,32,1024]{3,2,1,0:T(8,128)} %beta_ref.1, s32[256]{0:T(256)} %rows_ref.1, s32[256,1]{1,0:T(8,128)} %copy.9.owner_ref, s32[1,256]{1,0:T(1,128)} %bitcast.1, s32[256,128]{1,0:T(8,128)} %mask_ref.1, ...), custom_call_target="tpu_custom_call" | custom-call | tf_op jit(solution)/shard_map/pallas_call | solution.py:389
  69.4 2.3 %copy.12 = f32[8,32,1024]{2,1,0:T(8,128)} copy(f32[8,32,1024]{2,1,0:T(8,128)} %get-tuple-element.4) | data formatting | bytes 2097152
  71.7 1.8 %copy.13 = f32[3,256,128]{2,1,0:T(8,128)} copy(f32[3,256,128]{2,1,0:T(8,128)} %get-tuple-element.5) | data formatting | bytes 786432

commit v2 on v1

--- a/solution.py
+++ b/solution.py
@@ -36,11 +36,20 @@
     return value
 
 
+def picked_sum(selector, rows):
+    high = rows.astype(jnp.bfloat16)
+    rest = rows - high.astype(jnp.float32)
+    middle = rest.astype(jnp.bfloat16)
+    low = (rest - middle.astype(jnp.float32)).astype(jnp.bfloat16)
+    parts = [jnp.dot(selector, part, preferred_element_type=jnp.float32) for part in (high, middle, low)]
+    return parts[0] + (parts[1] + parts[2])
+
+
 def kernel(
     n_x, n_y,
     grad_ref, beta_ref, rows_ref, owner_ref, slot_ref, mask_ref, heights_ref,
     out_ref, back_ref,
-    coeff, state, halo_x, halo_y, face_y, rim_x, rim_y, rim_face,
+    coeff, state, halo_x, halo_y, face_y, rim_x, rim_y, rim_face, face_coeff,
     flat, picked, place, send_rows, recv_rows, send_slots, recv_slots,
     rim_send, rim_recv, x_send, x_recv, y_send, y_recv, row_send, row_recv, slot_send, slot_recv,
 ):
@@ -77,22 +86,21 @@
         rim_face[x : x + 1, :] = beta_ref[1, x, Y - 1 : Y, :]
 
     owner = owner_ref[...]
-    peer_ids = lax.broadcasted_iota(jnp.int32, (tiles, peers), 1)
+    peer_ids = lax.broadcasted_iota(jnp.int32, (peers, tiles), 0)
     named = (owner == peer_ids).astype(jnp.float32)
-    before = lax.broadcasted_iota(jnp.int32, (tiles, tiles), 0)
-    after = lax.broadcasted_iota(jnp.int32, (tiles, tiles), 1)
-    earlier = (after < before).astype(jnp.float32)
-    counts = jnp.dot(earlier, named, preferred_element_type=jnp.float32, precision=EXACT)
-    position = jnp.sum(counts * named, axis=1, keepdims=True)
+    down = lax.broadcasted_iota(jnp.int32, (tiles, tiles), 0)
+    across = lax.broadcasted_iota(jnp.int32, (tiles, tiles), 1)
+    earlier = (down < across).astype(jnp.bfloat16)
+    counts = jnp.dot(named.astype(jnp.bfloat16), earlier, preferred_element_type=jnp.float32)
+    position = jnp.sum(counts * named, axis=0, keepdims=True)
     target = owner.astype(jnp.float32) * CAP + position
-    columns = lax.broadcasted_iota(jnp.int32, (tiles, peers * CAP), 1).astype(jnp.float32)
-    place[...] = (target == columns).astype(jnp.float32)
-    slot_row = slot_ref[...].astype(jnp.float32)
-    slot_column = jnp.sum(jnp.where(before == after, slot_row, 0.0), axis=1, keepdims=True)
-    lanes = lax.broadcasted_iota(jnp.int32, (tiles, LANES), 1).astype(jnp.float32)
-    spread = jnp.where(position == lanes, slot_column, 0.0)
+    spots = lax.broadcasted_iota(jnp.int32, (peers * CAP, tiles), 0).astype(jnp.float32)
+    place[...] = (target == spots).astype(jnp.float32).astype(jnp.bfloat16)
+    spread = lax.broadcasted_iota(jnp.int32, (LANES, tiles), 0).astype(jnp.float32)
+    spread = (spread == position).astype(jnp.float32)
     slot_rows = lax.dot_general(
-        named, spread, (((0,), (0,)), ((), ())), preferred_element_type=jnp.float32, precision=EXACT
+        named * slot_ref[...].astype(jnp.float32), spread, (((1,), (1,)), ((), ())),
+        preferred_element_type=jnp.float32, precision=EXACT,
     )
     send_slots[...] = slot_rows.reshape(peers, 1, LANES)
 
@@ -160,8 +168,6 @@
 
     def from_above(tile, row):
         return jnp.where(row_ids == ROWS - 1, row, pltpu.roll(tile, ROWS - 1, 0))
-
-    first = omega_at(0)
 
     def prepare(x, g):
         r = slice(g * ROWS, (g + 1) * ROWS)
@@ -173,10 +179,15 @@
         inv = 1.0 / (up_x + low_x + up_y + low_y + up_z + low_z)
         up_z = jnp.where(z_ids == Z - 1, 0.0, up_z)
         for index, value in enumerate((up_x, low_x, up_y, low_y, up_z, low_z)):
-            coeff[index, x, r, :] = value * inv
+            value = value * inv
+            coeff[index, x, r, :] = value
+            if index == 3 and g == 0:
+                face_coeff[0, x : x + 1, :] = value[:1, :]
+            if index == 2 and g == groups - 1:
+                face_coeff[1, x : x + 1, :] = value[ROWS - 1 :, :]
         value = inv * grad_ref[x, r, :]
         state[0, x, r, :] = value
-        out_ref[x, r, :] = first * value
+        out_ref[x, r, :] = jnp.zeros_like(value)
         if g == 0:
             face_y[0, 0, x : x + 1, :] = value[:1, :]
         if g == groups - 1:
@@ -232,31 +243,47 @@
 
     total = ITERS * STEPS
 
-    def update(par, omega, weight, x, g):
+    def faces_of(par, value, x, g):
+        if g == 0:
+            face_y[par, 0, x : x + 1, :] = value[:1, :]
+        if g == groups - 1:
+            face_y[par, 1, x : x + 1, :] = value[ROWS - 1 :, :]
+
+    def update(par, omega, x, g):
         r = slice(g * ROWS, (g + 1) * ROWS)
         s = state[par, x, r, :]
-        above_x = halo_x[par, 1, r, :] if x == X - 1 else state[par, x + 1, r, :]
-        below_x = halo_x[par, 0, r, :] if x == 0 else state[par, x - 1, r, :]
+        out_ref[x, r, :] += omega * s
         if g == groups - 1:
-            above_row = halo_y[par, 1, x : x + 1, :]
+            above_row = 0.0
         else:
             above_row = state[par, x, (g + 1) * ROWS : (g + 1) * ROWS + 1, :]
         if g == 0:
-            below_row = halo_y[par, 0, x : x + 1, :]
+            below_row = 0.0
         else:
             below_row = state[par, x, g * ROWS - 1 : g * ROWS, :]
-        beside = coeff[0, x, r, :] * above_x + coeff[1, x, r, :] * below_x
-        beside += coeff[2, x, r, :] * from_above(s, above_row)
+        beside = coeff[2, x, r, :] * from_above(s, above_row)
         beside += coeff[3, x, r, :] * from_below(s, below_row)
         beside += coeff[4, x, r, :] * pltpu.roll(s, Z - 1, 1)
         beside += coeff[5, x, r, :] * pltpu.roll(s, 1, 1)
+        if x < X - 1:
+            beside += coeff[0, x, r, :] * state[par, x + 1, r, :]
+        if x > 0:
+            beside += coeff[1, x, r, :] * state[par, x - 1, r, :]
         value = s + omega * (beside - s)
         state[1 - par, x, r, :] = value
-        out_ref[x, r, :] += weight * value
-        if g == 0:
-            face_y[1 - par, 0, x : x + 1, :] = value[:1, :]
-        if g == groups - 1:
-            face_y[1 - par, 1, x : x + 1, :] = value[ROWS - 1 :, :]
+        if 0 < x < X - 1:
+            faces_of(1 - par, value, x, g)
+
+    def add_halo_x(par, omega, side, g):
+        @pl.when(has_x[side])
+        def _():
+            x_arrival(par, side, g).wait_recv()
+
+        x = (X - 1) * side
+        r = slice(g * ROWS, (g + 1) * ROWS)
+        value = state[1 - par, x, r, :] + omega * (coeff[1 - side, x, r, :] * halo_x[par, side, r, :])
+        state[1 - par, x, r, :] = value
+        faces_of(1 - par, value, x, g)
 
     def finish_sends(par, go):
         for side in range(2):
@@ -271,49 +298,57 @@
 
     def step_body(step, carry):
         par = step % 2
-        omega, weight = omega_at(step), omega_at(step + 1)
+        omega = omega_at(step)
         more = step + 2 < total
         finish_sends(1 - par, step > 0)
-
-        def ends(g):
+        for x in range(X):
+            for g in range(groups):
+                update(par, omega, x, g)
+
+        def send_x(side, g):
+            @pl.when(jnp.logical_and(has_x[side], more))
+            def _():
+                x_copy(1 - par, side, g).start()
+
+        for g in range(1, groups - 1):
             for side in range(2):
-                @pl.when(has_x[side])
-                def _():
-                    x_arrival(par, side, g).wait_recv()
-
-                update(par, omega, weight, (X - 1) * side, g)
-
-                @pl.when(jnp.logical_and(has_x[side], more))
-                def _():
-                    x_copy(1 - par, side, g).start()
-
-        for g in range(1, groups - 1):
-            ends(g)
-        for side, g in ((0, 0), (1, groups - 1)):
+                add_halo_x(par, omega, side, g)
+                send_x(side, g)
+        ends = (0, groups - 1)
+        for g in ends:
+            for side in range(2):
+                add_halo_x(par, omega, side, g)
+        for side in range(2):
             @pl.when(has_y[side])
             def _():
                 y_arrival(par, side).wait_recv()
 
-            ends(g)
-            for x in range(1, X - 1):
-                update(par, omega, weight, x, g)
+            face = face_y[1 - par, side] + omega * (face_coeff[side] * halo_y[par, side])
+            face_y[1 - par, side] = face
 
             @pl.when(jnp.logical_and(has_y[side], more))
             def _():
                 y_copy(1 - par, side).start()
 
-        for x in range(1, X - 1):
-            for g in range(1, groups - 1):
-                update(par, omega, weight, x, g)
+            row = (Y - 1) * side
+            for x in range(X):
+                state[1 - par, x, row : row + 1, :] = face[x : x + 1, :]
+            for x_side in range(2):
+                send_x(x_side, ends[side])
         return carry
 
     lax.fori_loop(0, total - 1, step_body, 0)
     finish_sends((total - 2) % 2, True)
+
+    last = omega_of(STEPS - 1 - (total - 1) % STEPS)
 
     for x in range(X):
         for b in range(blocks):
             start = (x * blocks + b) * Y
-            flat[start : start + Y, :] = out_ref[x, :, b * LANES : (b + 1) * LANES]
+            cut = slice(b * LANES, (b + 1) * LANES)
+            value = out_ref[x, :, cut] + last * state[(total - 1) % 2, x, :, cut]
+            out_ref[x, :, cut] = value
+            flat[start : start + Y, :] = value
 
     unroll = 8
 
@@ -322,16 +357,13 @@
         for lane in range(unroll):
             t = chunk * unroll + lane
             row = rows_ref[t]
-            x = row // (Y * blocks)
-            y = (row // blocks) % Y
-            at = (x * blocks + row % blocks) * Y + y
+            line = lax.div(row, blocks)
+            x = lax.div(line, Y)
+            at = (x * blocks + row - line * blocks) * Y + line - x * Y
             picked[pl.ds(t, 1), :] = flat[pl.ds(at, 1), :]
 
     jumps = picked[...] * mask_ref[...].astype(jnp.float32)
-    send_rows[...] = lax.dot_general(
-        place[...], jumps, (((0,), (0,)), ((), ())),
-        preferred_element_type=jnp.float32, precision=EXACT,
-    ).reshape(peers, CAP, LANES)
+    send_rows[...] = picked_sum(place[...], jumps).reshape(peers, CAP, LANES)
 
     @pl.loop(1, peers)
     def _(step):
@@ -352,7 +384,7 @@
     slot_of = jnp.sum(jnp.where(own == lane_ids, got, 0.0), axis=2, keepdims=True)
     slot_of = slot_of.reshape(peers * CAP, 1)
     slot_ids = lax.broadcasted_iota(jnp.int32, (peers * CAP, slots), 1).astype(jnp.float32)
-    chosen = (slot_of == slot_ids).astype(jnp.float32)
+    chosen = (slot_of == slot_ids).astype(jnp.float32).T.astype(jnp.bfloat16)
 
     slope = 0.5 * (heights_ref[2] - heights_ref[0])
     bend = heights_ref[2] - 2.0 * heights_ref[1] + heights_ref[0]
@@ -367,10 +399,7 @@
             send_rows.at[peer], recv_rows.at[peer], row_send.at[peer], row_recv.at[peer],
             device_id=place_of, device_id_type=MESH).wait()
 
-    table = lax.dot_general(
-        chosen, recv_rows[...].reshape(peers * CAP, LANES), (((0,), (0,)), ((), ())),
-        preferred_element_type=jnp.float32, precision=EXACT,
-    )
+    table = picked_sum(chosen, recv_rows[...].reshape(peers * CAP, LANES))
     back_ref[0] = table * (factor - 0.5 * skew)
     back_ref[1] = -2.0 * table * factor
     back_ref[2] = table * (factor + 0.5 * skew)
@@ -403,9 +432,10 @@
             pltpu.VMEM((Y, Z), f32),
             pltpu.VMEM((X, Z), f32),
             pltpu.VMEM((X, Z), f32),
+            pltpu.VMEM((2, X, Z), f32),
             pltpu.VMEM((X * Y * Z // LANES, LANES), f32),
             pltpu.VMEM((tiles, LANES), f32),
-            pltpu.VMEM((tiles, peers * CAP), f32),
+            pltpu.VMEM((peers * CAP, tiles), jnp.bfloat16),
             pltpu.VMEM((peers, CAP, LANES), f32),
             pltpu.VMEM((peers, CAP, LANES), f32),
             pltpu.VMEM((peers, 1, LANES), f32),
@@ -422,9 +452,9 @@
             dma((peers,)),
         ],
         compiler_params=pltpu.CompilerParams(
-            collective_id=0, has_side_effects=True, vmem_limit_bytes=56 * 1024 * 1024
+            collective_id=0, has_side_effects=True, vmem_limit_bytes=32 * 1024 * 1024
         ),
-    )(grad_pressure, beta, tile_rows, tile_owner, tile_slot.reshape(1, -1), face_mask, heights)
+    )(grad_pressure, beta, tile_rows, tile_owner.reshape(1, -1), tile_slot.reshape(1, -1), face_mask, heights)
 
 
 def solution(mesh):

time: 73.7 us -> 66.9 us (0.908)
  Pallas kernels: 67.3 us -> 57.2 us
  local copies, waits for them, and re-layouts: 5.55 us -> 8.76 us
    pallas_call x1, Pallas kernels: 67.3 us -> 57.2 us  [shards(): pl.pallas_call(functools.partial(kernel, n_x, n_y), out_shape=(jax.ShapeD...]
    unnamed x3 -> x16, local copies, waits for them, and re-layouts: 5.55 us -> 8.76 us
where the time goes in v2:
time: 66.9 us; the launch traced here: 66.6 us
  Pallas kernels  57.2 us (86%)
  local copies, waits for them, and re-layouts  8.76 us (13%)
    pallas_call x1, Pallas kernels, shards(): pl.pallas_call(functools.partial(kernel, n_x, n_y), out_shape=(jax.ShapeD...  57.2 us
    unnamed x16, local copies, waits for them, and re-layouts  8.76 us

profile of v2, /device:TPU:0, one launch (start us, length us, event | category | flops | bytes accessed | tf_op | source)
XLA Modules:
  0.0 66.6 jit_solution(5004105103009429141)
XLA Ops:
  0.6 0.0 copy-start
  0.6 1.9 %copy-done = f32[3,8,32,1024]{3,2,1,0:T(8,128)S(1)} copy-done((f32[3,8,32,1024]{3,2,1,0:T(8,128)S(1)}, f32[3,8,32,1024]{3,2,1,0:T(8,128)}, u32[]{:S(2)}) %copy-start) | copy-done | bytes 3145752
  2.5 0.0 copy-start.1
  2.5 1.2 %copy-done.1 = f32[8,32,1024]{2,1,0:T(8,128)S(1)} copy-done((f32[8,32,1024]{2,1,0:T(8,128)S(1)}, f32[8,32,1024]{2,1,0:T(8,128)}, u32[]{:S(2)}) %copy-start.1) | copy-done | bytes 1048600
  3.7 0.0 copy-start.2
  3.8 1.0 %copy-done.2 = f32[3,256,128]{2,1,0:T(8,128)S(1)} copy-done((f32[3,256,128]{2,1,0:T(8,128)S(1)}, f32[3,256,128]{2,1,0:T(8,128)}, u32[]{:S(2)}) %copy-start.2) | copy-done | bytes 393240
  4.7 0.0 copy-start.3
  4.7 0.9 %copy-done.3 = s32[256,128]{1,0:T(8,128)S(1)} copy-done((s32[256,128]{1,0:T(8,128)S(1)}, s32[256,128]{1,0:T(8,128)}, u32[]{:S(2)}) %copy-start.3) | copy-done | bytes 131096
  5.6 0.0 copy-start.4
  5.7 0.7 %copy-done.4 = s32[256]{0:T(256)S(1)} copy-done((s32[256]{0:T(256)S(1)}, s32[256]{0:T(256)}, u32[]{:S(2)}) %copy-start.4) | copy-done | bytes 1048
  6.3 0.0 copy-start.5
  6.3 0.7 %copy-done.5 = s32[256,1]{0,1:T(1,128)S(1)} copy-done((s32[256,1]{0,1:T(1,128)S(1)}, s32[256,1]{0,1:T(1,128)}, u32[]{:S(2)}) %copy-start.5) | copy-done | bytes 1048
  7.0 0.0 copy-start.6
  7.0 0.7 %copy-done.6 = s32[256]{0:T(256)S(1)} copy-done((s32[256]{0:T(256)S(1)}, s32[256]{0:T(256)}, u32[]{:S(2)}) %copy-start.6) | copy-done | bytes 1048
  7.7 57.2 %shard_map.86 = (f32[8,32,1024]{2,1,0:T(8,128)S(1)}, f32[3,256,128]{2,1,0:T(8,128)S(1)}) custom-call(f32[8,32,1024]{2,1,0:T(8,128)S(1)} %copy-done.1, f32[3,8,32,1024]{3,2,1,0:T(8,128)S(1)} %copy-done, s32[256]{0:T(256)S(1)} %copy-done.4, s32[1,256]{1,0:T(1,128)S(1)} %bitcast.2, s32[1,256]{1,0:T(1,128)S(1)} %bitcast.3, s32[256,128]{1,0:T(8,128)S(1)} %copy-done.3, ...), custom_call_target="tpu_custom_call" | custom-call | tf_op jit(solution)/shard_map/pallas_call | solution.py:418
  64.9 1.0 %copy.11 = f32[8,32,1024]{2,1,0:T(8,128)} copy(f32[8,32,1024]{2,1,0:T(8,128)S(1)} %get-tuple-element.4) | data formatting | bytes 2097152
  65.9 0.7 %copy.12 = f32[3,256,128]{2,1,0:T(8,128)} copy(f32[3,256,128]{2,1,0:T(8,128)S(1)} %get-tuple-element.5) | data formatting | bytes 786432
Async XLA Ops:
  0.6 1.9 %copy-start = (f32[3,8,32,1024]{3,2,1,0:T(8,128)S(1)}, f32[3,8,32,1024]{3,2,1,0:T(8,128)}, u32[]{:S(2)}) copy-start(f32[3,8,32,1024]{3,2,1,0:T(8,128)} %beta_ref.1) | copy-start | bytes 9437188
  2.5 1.2 %copy-start.1 = (f32[8,32,1024]{2,1,0:T(8,128)S(1)}, f32[8,32,1024]{2,1,0:T(8,128)}, u32[]{:S(2)}) copy-start(f32[8,32,1024]{2,1,0:T(8,128)} %grad_ref.1) | copy-start | bytes 3145732
  3.7 1.0 %copy-start.2 = (f32[3,256,128]{2,1,0:T(8,128)S(1)}, f32[3,256,128]{2,1,0:T(8,128)}, u32[]{:S(2)}) copy-start(f32[3,256,128]{2,1,0:T(8,128)} %heights_ref.1) | copy-start | bytes 1179652
  4.7 0.9 %copy-start.3 = (s32[256,128]{1,0:T(8,128)S(1)}, s32[256,128]{1,0:T(8,128)}, u32[]{:S(2)}) copy-start(s32[256,128]{1,0:T(8,128)} %mask_ref.1) | copy-start | bytes 393220
  5.6 0.7 %copy-start.4 = (s32[256]{0:T(256)S(1)}, s32[256]{0:T(256)}, u32[]{:S(2)}) copy-start(s32[256]{0:T(256)} %rows_ref.1) | copy-start | bytes 3076
  6.3 0.7 %copy-start.5 = (s32[256,1]{0,1:T(1,128)S(1)}, s32[256,1]{0,1:T(1,128)}, u32[]{:S(2)}) copy-start(s32[256,1]{0,1:T(1,128)} %param.10) | copy-start | bytes 3076
  7.0 0.7 %copy-start.6 = (s32[256]{0:T(256)S(1)}, s32[256]{0:T(256)}, u32[]{:S(2)}) copy-start(s32[256]{0:T(256)} %param.11) | copy-start | bytes 3076

commit v3 on v2

--- a/solution.py
+++ b/solution.py
@@ -47,8 +47,10 @@
 
 def kernel(
     n_x, n_y,
-    grad_ref, beta_ref, rows_ref, owner_ref, slot_ref, mask_ref, heights_ref,
-    out_ref, back_ref,
+    grad_in, beta_in, rows_in, owner_in, slot_in, mask_in, heights_in,
+    out_hbm, back_ref,
+    out_ref,
+    grad_ref, beta_ref, rows_ref, owner_ref, slot_ref, mask_ref, heights_ref, load_sem,
     coeff, state, halo_x, halo_y, face_y, rim_x, rim_y, rim_face, face_coeff,
     flat, picked, place, send_rows, recv_rows, send_slots, recv_slots,
     rim_send, rim_recv, x_send, x_recv, y_send, y_recv, row_send, row_recv, slot_send, slot_recv,
@@ -82,8 +84,19 @@
     def _(step):
         pl.semaphore_signal(barrier, inc=1, device_id=peer_at(step)[1], device_id_type=MESH)
 
-    for x in range(X):
-        rim_face[x : x + 1, :] = beta_ref[1, x, Y - 1 : Y, :]
+    names = ("owner", "slot", "beta", "grad", "rows", "mask", "heights")
+    pairs = (
+        (owner_in, owner_ref), (slot_in, slot_ref), (beta_in, beta_ref), (grad_in, grad_ref),
+        (rows_in, rows_ref), (mask_in, mask_ref), (heights_in, heights_ref),
+    )
+    loads = {
+        name: pltpu.make_async_copy(source, held, load_sem.at[index])
+        for index, (name, (source, held)) in enumerate(zip(names, pairs))
+    }
+    for name in names:
+        loads[name].start()
+    for name in ("owner", "slot"):
+        loads[name].wait()
 
     owner = owner_ref[...]
     peer_ids = lax.broadcasted_iota(jnp.int32, (peers, tiles), 0)
@@ -103,6 +116,10 @@
         preferred_element_type=jnp.float32, precision=EXACT,
     )
     send_slots[...] = slot_rows.reshape(peers, 1, LANES)
+
+    loads["beta"].wait()
+    for x in range(X):
+        rim_face[x : x + 1, :] = beta_ref[1, x, Y - 1 : Y, :]
 
     pl.semaphore_wait(barrier, peers - 1)
 
@@ -193,6 +210,7 @@
         if g == groups - 1:
             face_y[0, 1, x : x + 1, :] = value[ROWS - 1 :, :]
 
+    loads["grad"].wait()
     for x in range(1, X):
         for g in range(1, groups):
             prepare(x, g)
@@ -339,6 +357,8 @@
 
     lax.fori_loop(0, total - 1, step_body, 0)
     finish_sends((total - 2) % 2, True)
+    for name in ("rows", "mask", "heights"):
+        loads[name].wait()
 
     last = omega_of(STEPS - 1 - (total - 1) % STEPS)
 
@@ -350,6 +370,8 @@
             out_ref[x, :, cut] = value
             flat[start : start + Y, :] = value
 
+    store = pltpu.make_async_copy(out_ref, out_hbm, load_sem.at[7])
+    store.start()
     unroll = 8
 
     @pl.loop(0, tiles // unroll)
@@ -403,6 +425,7 @@
     back_ref[0] = table * (factor - 0.5 * skew)
     back_ref[1] = -2.0 * table * factor
     back_ref[2] = table * (factor + 0.5 * skew)
+    store.wait()
 
 
 def shards(grad_pressure, beta, tile_rows, tile_owner, tile_slot, face_mask, heights):
@@ -413,7 +436,7 @@
     tiles = tile_rows.shape[0]
     f32 = jnp.float32
     vmem = pl.BlockSpec(memory_space=pltpu.VMEM)
-    smem = pl.BlockSpec(memory_space=pltpu.SMEM)
+    hbm = pl.BlockSpec(memory_space=pltpu.HBM)
     dma = pltpu.SemaphoreType.DMA
     return pl.pallas_call(
         functools.partial(kernel, n_x, n_y),
@@ -421,9 +444,18 @@
             jax.ShapeDtypeStruct((X, Y, Z), f32),
             jax.ShapeDtypeStruct(heights.shape, f32),
         ),
-        in_specs=[vmem, vmem, smem, vmem, vmem, vmem, vmem],
-        out_specs=(vmem, vmem),
+        in_specs=[hbm] * 7,
+        out_specs=(hbm, vmem),
         scratch_shapes=[
+            pltpu.VMEM((X, Y, Z), f32),
+            pltpu.VMEM((X, Y, Z), f32),
+            pltpu.VMEM(beta.shape, f32),
+            pltpu.SMEM((tiles,), jnp.int32),
+            pltpu.VMEM((1, tiles), jnp.int32),
+            pltpu.VMEM((1, tiles), jnp.int32),
+            pltpu.VMEM(face_mask.shape, jnp.int32),
+            pltpu.VMEM(heights.shape, f32),
+            dma((8,)),
             pltpu.VMEM((6, X, Y, Z), f32),
             pltpu.VMEM((2, X, Y, Z), f32),
             pltpu.VMEM((2, 2, Y, Z), f32),
@@ -452,7 +484,7 @@
             dma((peers,)),
         ],
         compiler_params=pltpu.CompilerParams(
-            collective_id=0, has_side_effects=True, vmem_limit_bytes=32 * 1024 * 1024
+            collective_id=0, has_side_effects=True, vmem_limit_bytes=56 * 1024 * 1024
         ),
     )(grad_pressure, beta, tile_rows, tile_owner.reshape(1, -1), tile_slot.reshape(1, -1), face_mask, heights)
 

time: 66.9 us -> 62.4 us (0.933)
  local copies, waits for them, and re-layouts: 8.76 us -> 4.07 us
    unnamed x16 -> x2, local copies, waits for them, and re-layouts: 8.76 us -> 4.07 us
where the time goes in v3:
time: 62.4 us; the launch traced here: 62.2 us
  Pallas kernels  57.5 us (92%)
  local copies, waits for them, and re-layouts  4.07 us (7%)
  between operations  0.64 us (1%)
    pallas_call x1, Pallas kernels, shards(): pl.pallas_call(functools.partial(kernel, n_x, n_y), out_shape=(jax.ShapeD...  57.5 us
    unnamed x2, local copies, waits for them, and re-layouts  4.07 us

profile of v3, /device:TPU:0, one launch (start us, length us, event | category | flops | bytes accessed | tf_op | source)
XLA Modules:
  0.0 62.2 jit_solution(9641379106603574635)
XLA Ops:
  0.6 57.5 %shard_map.86 = (f32[8,32,1024]{2,1,0:T(8,128)}, f32[3,256,128]{2,1,0:T(8,128)}) custom-call(f32[8,32,1024]{2,1,0:T(8,128)} %grad_in.1, f32[3,8,32,1024]{3,2,1,0:T(8,128)} %beta_in.1, s32[256]{0:T(256)} %rows_in.1, s32[1,256]{1,0:T(1,128)} %bitcast.2, s32[1,256]{1,0:T(1,128)} %bitcast.3, s32[256,128]{1,0:T(8,128)} %mask_in.1, f32[3,256,128]{2,1,0:T(8,128)} %heights_in.1), custom_call_target="tpu_custom_call" | custom-call | tf_op jit(solution)/shard_map/pallas_call | solution.py:441
  58.1 2.3 %copy.11 = f32[8,32,1024]{2,1,0:T(8,128)} copy(f32[8,32,1024]{2,1,0:T(8,128)} %get-tuple-element.4) | data formatting | bytes 2097152
  60.4 1.8 %copy.12 = f32[3,256,128]{2,1,0:T(8,128)} copy(f32[3,256,128]{2,1,0:T(8,128)} %get-tuple-element.5) | data formatting | bytes 786432
